TPU v7x, 32 devices: a whole 2x2x4 slice. The times are simulated.
32 devices in a mesh: seq: 32 (over z, y, x, core).
Axes of the slice: x: 2, y: 2, z: 4, core: 2. Of those that a mesh axis runs over, the one named last changes fastest.
Arguments:
- tokens: bfloat16 [65536, 320], P('seq'), may hold values from -6 to 6
- w_in: bfloat16 [2, 320, 640], replicated, may hold values from -0.3125 to 0.3125
- b_in: float32 [2, 640], replicated, may hold values from -3 to 3
- w_out: bfloat16 [2, 640, 320], replicated, may hold values from -0.25 to 0.25
- b_out: float32 [2, 320], replicated, may hold values from -3 to 3
- cotangent: bfloat16 [65536, 320], P('seq'), may hold values from -6 to 6
Outputs:
- result: bfloat16 [65536, 320], P('seq')
- grad_tokens: bfloat16 [65536, 320], P('seq')
- grad_w_in: float32 [2, 320, 640], replicated
- grad_b_in: float32 [2, 640], replicated
- grad_w_out: float32 [2, 640, 320], replicated
- grad_b_out: float32 [2, 320], replicated
All inputs are finite; a program needn't handle non-finite values.
Results may differ from a plain program's by a relative error of at most 0.0065.
Values may be sent and summed in bfloat16 or wider, within the bound.
A program may use at most 128 MiB of HBM per device.

v0:
```python
import functools

import jax
import jax.numpy as jnp
from jax import lax
from jax.experimental import pallas as pl
from jax.experimental.pallas import tpu as pltpu
from jax.sharding import PartitionSpec as P

TRACK_W = 16
LANES = 128
TILE = 512
MESH = pl.DeviceIdType.MESH


def plan(n, rows, width):
    tracks = width // TRACK_W
    total = rows * n
    shifts = [0] + [min(2 ** (t - 1), total // 2) for t in range(1, tracks)]
    near = [t for t in range(1, tracks) if shifts[t] < rows]
    small = [t for t in near if shifts[t] <= LANES]
    groups = []
    for t in range(1, tracks):
        if shifts[t] >= rows:
            hops = (shifts[t] // rows) % n
            if groups and groups[-1][0] == hops:
                groups[-1][2] = t + 1
            else:
                groups.append([hops, t, t + 1])
    return shifts, near, small, groups


def channels(first, last):
    return pl.ds(first * TRACK_W, (last - first) * TRACK_W)


class Rotation:
    def __init__(self, me, n, sign, src, dst, halo, send, recv):
        self.sign, self.src, self.dst, self.halo = sign, src, dst, halo
        width, rows = src.shape
        self.rows = rows
        self.shifts, self.near, self.small, self.groups = plan(n, rows, width)
        self.copies = []

        def add(source, target, hops):
            k = len(self.copies)
            self.copies.append(
                pltpu.make_async_remote_copy(
                    src_ref=source,
                    dst_ref=target,
                    send_sem=send.at[k],
                    recv_sem=recv.at[k],
                    device_id=(lax.rem(me + (sign * hops) % n, n),),
                    device_id_type=MESH,
                )
            )

        for hops, first, last in sorted(self.groups, reverse=True):
            piece = channels(first, last)
            add(src.at[piece, :], dst.at[piece, :], hops)
        wide = [t for t in self.near if t not in self.small]
        for first, last, size in [(t, t + 1, self.shifts[t]) for t in reversed(wide)] + [
            (self.small[0], self.small[-1] + 1, LANES)
        ]:
            start = rows - size if sign > 0 else 0
            piece = channels(first, last)
            add(src.at[piece, pl.ds(start, size)], halo.at[piece, pl.ds(0, size)], 1)

    def start(self):
        for copy in self.copies:
            copy.start()

    def finish(self):
        rows, src, dst, halo = self.rows, self.src, self.dst, self.halo
        for copy in self.copies:
            copy.wait()
        dst[channels(0, 1), :] = src[channels(0, 1), :]
        lane = lax.broadcasted_iota(jnp.int32, (TRACK_W, LANES), 1)
        for t in self.near:
            s, piece = self.shifts[t], channels(t, t + 1)
            if s % LANES == 0:
                if self.sign > 0:
                    dst[piece, pl.ds(s, rows - s)] = src[piece, pl.ds(0, rows - s)]
                    dst[piece, pl.ds(0, s)] = halo[piece, pl.ds(0, s)]
                else:
                    dst[piece, pl.ds(0, rows - s)] = src[piece, pl.ds(s, rows - s)]
                    dst[piece, pl.ds(rows - s, s)] = halo[piece, pl.ds(0, s)]
                continue
            body = src[piece, :].astype(jnp.float32)
            edge = halo[piece, pl.ds(0, LANES)].astype(jnp.float32)
            if self.sign > 0:
                body = pltpu.roll(body, s, 1)
                edge = pltpu.roll(edge, s, 1)
                first = jnp.where(lane < s, edge, body[:, :LANES])
                body = jnp.concatenate([first, body[:, LANES:]], axis=1)
            else:
                body = pltpu.roll(body, rows - s, 1)
                edge = pltpu.roll(edge, LANES - s, 1)
                last = jnp.where(lane >= LANES - s, edge, body[:, rows - LANES :])
                body = jnp.concatenate([body[:, : rows - LANES], last], axis=1)
            dst[piece, :] = body.astype(jnp.bfloat16)


def dot(a, b):
    return jnp.dot(a, b, preferred_element_type=jnp.float32)


def dot_t(a, b):
    return lax.dot_general(a, b, (((1,), (1,)), ((), ())), preferred_element_type=jnp.float32)


def gelu_both(t):
    c = 0.7978845608028654
    sq = t * t
    th = jnp.tanh(c * (t + 0.044715 * (sq * t)))
    half = 0.5 * (1.0 + th)
    slope = half + (0.5 * t) * ((1.0 - th * th) * (c + (3.0 * 0.044715 * c) * sq))
    return half * t, slope


def kernel(
    n, scale, u0, cot, w_in, w_in_t, w_out, w_out_t, b_in, b_out,
    result, grad, reduced,
    back1, m0, u1, m1, r1, g1, back0, halo, act, slope, delta, acc, part, land, own, fin,
    rot_send, rot_recv, rs_send, rs_recv, ag_send, ag_recv,
):
    me = lax.axis_index("seq")
    width, rows = u0.shape
    hidden = w_in_t.shape[1]
    chunk = part.shape[2]
    tile = min(TILE, rows)
    steps = rows // tile

    barrier = pltpu.get_barrier_semaphore()

    def greet(k, carry):
        pl.semaphore_signal(
            barrier, inc=1, device_id=(lax.rem(me + k, n),), device_id_type=MESH
        )
        return carry

    lax.fori_loop(1, n, greet, 0)
    acc[...] = jnp.zeros_like(acc)
    pl.semaphore_wait(barrier, n - 1)

    def rotation(i, sign, src, dst):
        return Rotation(me, n, sign, src, dst, halo.at[i], rot_send.at[i], rot_recv.at[i])

    rot_cot = rotation(0, -1, cot, back1)
    rot_m0 = rotation(1, 1, m0, u1)
    rot_m1 = rotation(2, 1, m1, r1)
    rot_g1 = rotation(3, -1, g1, back0)

    def tiles(body):
        def step(i, carry):
            body(pl.ds(pl.multiple_of(i * tile, tile), tile))
            return carry

        lax.fori_loop(0, steps, step, 0)

    def forward(l, u, out):
        def body(cols):
            x = u[:, cols]
            pre = dot(w_in_t[l], x) + b_in[l]
            a, d = gelu_both(pre)
            a = a.astype(jnp.bfloat16)
            act[l, :, cols] = a
            slope[l, :, cols] = d
            out[:, cols] = (x.astype(jnp.float32) + dot(w_out_t[l], a) + b_out[l]).astype(
                jnp.bfloat16
            )

        tiles(body)

    def backward(l, back, out):
        def body(cols):
            b = back[:, cols]
            d = (dot(w_out[l], b) * slope[l, :, cols]).astype(jnp.bfloat16)
            delta[:, cols] = d
            out[:, cols] = (b.astype(jnp.float32) + dot(w_in[l], d)).astype(jnp.bfloat16)

        tiles(body)

    def weight_grads(l, u, back):
        def body(cols):
            b, d = back[:, cols], delta[:, cols]
            acc[l, pl.ds(0, hidden), pl.ds(0, width)] += dot_t(act[l, :, cols], b)
            acc[l, pl.ds(hidden, hidden), pl.ds(0, width)] += dot_t(d, u[:, cols])
            acc[l, pl.ds(0, width), pl.ds(width, 1)] += jnp.sum(
                b.astype(jnp.float32), axis=1, keepdims=True
            )
            acc[l, pl.ds(hidden, hidden), pl.ds(width, 1)] += jnp.sum(
                d.astype(jnp.float32), axis=1, keepdims=True
            )

        tiles(body)

        def narrow(i, carry):
            part[l, i] = acc[l, pl.ds(pl.multiple_of(i * chunk, 8), chunk), :].astype(jnp.bfloat16)
            return carry

        lax.fori_loop(0, n, narrow, 0)

    def scatter(l, k):
        to = lax.rem(me + k, n)
        return pltpu.make_async_remote_copy(
            src_ref=part.at[l, to],
            dst_ref=land.at[l, k],
            send_sem=rs_send.at[l, k],
            recv_sem=rs_recv.at[l, k],
            device_id=(to,),
            device_id_type=MESH,
        )

    def gather(l, k):
        to = lax.rem(me + k, n)
        return pltpu.make_async_remote_copy(
            src_ref=own.at[l],
            dst_ref=fin.at[l, me],
            send_sem=ag_send.at[l, k],
            recv_sem=ag_recv.at[l, k],
            device_id=(to,),
            device_id_type=MESH,
        )

    def gathered(l, k):
        return pltpu.make_async_remote_copy(
            src_ref=own.at[l],
            dst_ref=fin.at[l, lax.rem(me + n - k, n)],
            send_sem=ag_send.at[l, k],
            recv_sem=ag_recv.at[l, k],
            device_id=(lax.rem(me + k, n),),
            device_id_type=MESH,
        )

    def each(body):
        def step(k, carry):
            body(k)
            return carry

        lax.fori_loop(1, n, step, 0)

    def scatter_start(l):
        each(lambda k: scatter(l, k).start())

    def reduce_and_gather(l):
        each(lambda k: scatter(l, k).wait())

        def add(k, total):
            return total + land[l, k].astype(jnp.float32)

        mine = acc[l, pl.ds(pl.multiple_of(me * chunk, 8), chunk), :]
        total = (lax.fori_loop(1, n, add, mine) * scale).astype(jnp.bfloat16)
        own[l] = total
        fin[l, me] = total
        each(lambda k: gather(l, k).start())

    def gather_finish(l):
        each(lambda k: gathered(l, k).wait())

    rot_cot.start()
    forward(0, u0, m0)
    rot_m0.start()
    rot_cot.finish()
    rot_m0.finish()
    forward(1, u1, m1)
    backward(1, back1, g1)
    rot_g1.start()
    rot_m1.start()
    weight_grads(1, u1, back1)
    rot_g1.finish()
    scatter_start(1)
    backward(0, back0, grad)
    weight_grads(0, u0, back0)
    scatter_start(0)
    rot_m1.finish()
    result[...] = r1[...]
    reduce_and_gather(1)
    reduce_and_gather(0)
    gather_finish(1)
    gather_finish(0)
    reduced[...] = fin[...]


def local(n, tokens, w_in, b_in, w_out, b_out, cotangent):
    rows, width = tokens.shape
    layers, _, hidden = w_in.shape
    scale = 1.0 / (rows * n) ** 0.5
    chunk = -(-2 * hidden // (8 * n)) * 8
    cols = -(-(width + 1) // LANES) * LANES
    shifts, near, small, groups = plan(n, rows, width)
    copies = len(groups) + len(near) - len(small) + 1
    bf16, f32 = jnp.bfloat16, jnp.float32
    vmem = pl.BlockSpec(memory_space=pltpu.VMEM)
    block = pltpu.VMEM((width, rows), bf16)
    result, grad, reduced = pl.pallas_call(
        functools.partial(kernel, n, scale),
        out_shape=[
            jax.ShapeDtypeStruct((width, rows), bf16),
            jax.ShapeDtypeStruct((width, rows), bf16),
            jax.ShapeDtypeStruct((layers, n, chunk, cols), bf16),
        ],
        in_specs=[vmem] * 8,
        out_specs=[vmem] * 3,
        scratch_shapes=[block] * 7
        + [
            pltpu.VMEM((4, (near[-1] + 1) * TRACK_W, rows // 2), bf16),
            pltpu.VMEM((layers, hidden, rows), bf16),
            pltpu.VMEM((layers, hidden, rows), f32),
            pltpu.VMEM((hidden, rows), bf16),
            pltpu.VMEM((layers, n * chunk, cols), f32),
            pltpu.VMEM((layers, n, chunk, cols), bf16),
            pltpu.VMEM((layers, n, chunk, cols), bf16),
            pltpu.VMEM((layers, chunk, cols), bf16),
            pltpu.VMEM((layers, n, chunk, cols), bf16),
            pltpu.SemaphoreType.DMA((4, copies)),
            pltpu.SemaphoreType.DMA((4, copies)),
        ]
        + [pltpu.SemaphoreType.DMA((layers, n))] * 4,
        compiler_params=pltpu.CompilerParams(
            collective_id=0, has_side_effects=True, vmem_limit_bytes=64 * 1024 * 1024 - 65536
        ),
    )(
        tokens.T,
        cotangent.T,
        w_in,
        w_in.transpose(0, 2, 1),
        w_out,
        w_out.transpose(0, 2, 1),
        b_in[:, :, None],
        b_out[:, :, None],
    )
    sums = reduced.reshape(layers, n * chunk, cols).astype(f32)
    return (
        result.T,
        grad.T,
        sums[:, hidden : 2 * hidden, :width].transpose(0, 2, 1),
        sums[:, hidden : 2 * hidden, width],
        sums[:, :hidden, :width],
        sums[:, :width, width],
    )


def solution(mesh):
    return jax.shard_map(
        functools.partial(local, mesh.shape["seq"]),
        mesh=mesh,
        in_specs=(P("seq", None), P(), P(), P(), P(), P("seq", None)),
        out_specs=(P("seq", None), P("seq", None), P(), P(), P(), P()),
        check_vma=False,
    )
```

profile of v0, /device:TPU:15, one launch (start us, length us, event | category | flops | bytes accessed | tf_op | source)
XLA Modules:
  0.0 194.1 jit_solution(16289121709292585535)
XLA Ops:
  0.6 0.0 copy-start.1
  0.6 1.7 copy.21.b_out
  2.3 1.8 copy.20.b_in
  4.1 2.2 %copy.18 = bf16[2,320,640]{1,2,0:T(8,128)(2,1)} copy(bf16[2,320,640]{2,1,0:T(8,128)(2,1)} %w_in.1) | data formatting | bytes 1638400 | tf_op args[1]
  6.3 0.0 copy-done.1
  6.3 1.3 copy.19.w_out
  7.6 168.9 %shard_map.109 = (bf16[320,2048]{1,0:T(8,128)(2,1)}, bf16[320,2048]{1,0:T(8,128)(2,1)}, bf16[2,32,40,384]{3,2,1,0:T(8,128)(2,1)}) custom-call(bf16[320,2048]{1,0:T(8,128)(2,1)} %bitcast.17, bf16[320,2048]{1,0:T(8,128)(2,1)} %bitcast.18, bf16[2,320,640]{2,1,0:T(8,128)(2,1)} %w_in.1, bf16[2,640,320]{2,1,0:T(8,128)(2,1)} %bitcast.14, ...), custom_call_target="tpu_custom_call" | custom-call | tf_op jit(solution)/shard_map/pallas_call | solution.py:296
  176.5 1.8 bitcast_convert_fusion
  178.3 0.0 copy-start
  178.3 1.9 copy-done
  180.1 0.1 slice.19
  180.3 0.7 copy.29
  181.0 1.3 slice.17
  182.4 0.8 copy.27
  183.2 3.7 %fusion = (f32[2,640,320]{2,1,0:T(8,128)}, f32[2,640,320]{2,1,0:T(8,128)S(1)}) fusion(f32[2,1280,384]{2,1,0:T(8,128)} %copy-done), kind=kLoop, calls=%fused_computation.1 | loop fusion | bytes 6553600 | tf_op jit(solution)/shard_map/slice | solution.py:339
  186.9 2.7 %copy.28 = f32[2,640,320]{1,2,0:T(8,128)} copy(f32[2,640,320]{2,1,0:T(8,128)} %get-tuple-element.12) | data formatting | bytes 3276800
  189.6 0.0 copy-start.3
  189.6 1.7 copy.26
  191.3 0.0 copy-start.2
  191.3 0.0 copy-done.3
  191.3 1.1 copy.32
  192.3 0.7 copy-done.2
  193.1 1.1 copy.33
Async XLA Ops:
  0.6 5.7 %copy-start.1 = (bf16[2,640,320]{1,2,0:T(8,128)(2,1)S(1)}, bf16[2,640,320]{1,2,0:T(8,128)(2,1)}, u32[]{:S(2)}) copy-start(bf16[2,640,320]{1,2,0:T(8,128)(2,1)} %param.9) | copy-start | bytes 2457604
  178.3 1.9 copy-start
  189.6 1.7 copy-start.3
  191.3 1.8 copy-start.2
where the time goes:
time: 194 us
  Pallas kernels  169 us (87%)
  local copies, waits for them, and re-layouts  22.8 us (12%)
    pallas_call x1, Pallas kernels, local(): pl.pallas_call(functools.partial(kernel, n, scale), out_shape=[jax.ShapeD...  169 us
    unnamed x16, local copies, waits for them, and re-layouts  14.2 us

commit v1 on v0

--- a/solution.py
+++ b/solution.py
@@ -119,15 +119,16 @@
 
 
 def kernel(
-    n, scale, u0, cot, w_in, w_in_t, w_out, w_out_t, b_in, b_out,
+    n, scale, u0, cot, w_in, w_out_t, b_in_row, b_out_row,
     result, grad, reduced,
-    back1, m0, u1, m1, r1, g1, back0, halo, act, slope, delta, acc, part, land, own, fin,
+    back1, m0, u1, m1, r1, g1, back0, w_in_t, w_out, b_in, b_out,
+    halo, act, slope, delta, acc, part, land, own, fin,
     rot_send, rot_recv, rs_send, rs_recv, ag_send, ag_recv,
 ):
     me = lax.axis_index("seq")
     width, rows = u0.shape
-    hidden = w_in_t.shape[1]
-    chunk = part.shape[2]
+    layers, hidden, _ = w_in_t.shape
+    owners, chunk = part.shape[1:3]
     tile = min(TILE, rows)
     steps = rows // tile
 
@@ -141,6 +142,12 @@
 
     lax.fori_loop(1, n, greet, 0)
     acc[...] = jnp.zeros_like(acc)
+    for l in range(layers):
+        w_in_t[l] = w_in[l].T
+        w_out[l] = w_out_t[l].T
+        for row, column in ((b_in_row, b_in), (b_out_row, b_out)):
+            spread = jnp.broadcast_to(row[l : l + 1, :], (LANES, row.shape[1]))
+            column[l] = spread.T[:, :1]
     pl.semaphore_wait(barrier, n - 1)
 
     def rotation(i, sign, src, dst):
@@ -182,16 +189,15 @@
         tiles(body)
 
     def weight_grads(l, u, back):
+        ones = jnp.ones((TRACK_W, tile), jnp.bfloat16)
+
         def body(cols):
             b, d = back[:, cols], delta[:, cols]
-            acc[l, pl.ds(0, hidden), pl.ds(0, width)] += dot_t(act[l, :, cols], b)
-            acc[l, pl.ds(hidden, hidden), pl.ds(0, width)] += dot_t(d, u[:, cols])
-            acc[l, pl.ds(0, width), pl.ds(width, 1)] += jnp.sum(
-                b.astype(jnp.float32), axis=1, keepdims=True
+            acc[l, pl.ds(0, width), :] += dot_t(b, act[l, :, cols])
+            acc[l, pl.ds(width, width + TRACK_W), :] += dot_t(
+                jnp.concatenate([u[:, cols], ones], axis=0), d
             )
-            acc[l, pl.ds(hidden, hidden), pl.ds(width, 1)] += jnp.sum(
-                d.astype(jnp.float32), axis=1, keepdims=True
-            )
+            acc[l, pl.ds(2 * width + TRACK_W, 8), pl.ds(0, width)] += dot_t(ones, b)[:8]
 
         tiles(body)
 
@@ -199,7 +205,7 @@
             part[l, i] = acc[l, pl.ds(pl.multiple_of(i * chunk, 8), chunk), :].astype(jnp.bfloat16)
             return carry
 
-        lax.fori_loop(0, n, narrow, 0)
+        lax.fori_loop(0, owners, narrow, 0)
 
     def scatter(l, k):
         to = lax.rem(me + k, n)
@@ -212,21 +218,20 @@
             device_id_type=MESH,
         )
 
-    def gather(l, k):
-        to = lax.rem(me + k, n)
+    def incoming(l, k):
         return pltpu.make_async_remote_copy(
             src_ref=own.at[l],
-            dst_ref=fin.at[l, me],
-            send_sem=ag_send.at[l, k],
-            recv_sem=ag_recv.at[l, k],
-            device_id=(to,),
+            dst_ref=land.at[l, k],
+            send_sem=rs_send.at[l, k],
+            recv_sem=rs_recv.at[l, k],
+            device_id=(lax.rem(me + k, n),),
             device_id_type=MESH,
         )
 
-    def gathered(l, k):
+    def gather(l, k, slot):
         return pltpu.make_async_remote_copy(
             src_ref=own.at[l],
-            dst_ref=fin.at[l, lax.rem(me + n - k, n)],
+            dst_ref=fin.at[l, slot],
             send_sem=ag_send.at[l, k],
             recv_sem=ag_recv.at[l, k],
             device_id=(lax.rem(me + k, n),),
@@ -240,23 +245,46 @@
 
         lax.fori_loop(1, n, step, 0)
 
+    def to_owner(body):
+        def guarded(k):
+            @pl.when(lax.rem(me + k, n) < owners)
+            def _():
+                body(k)
+
+        each(guarded)
+
     def scatter_start(l):
-        each(lambda k: scatter(l, k).start())
+        to_owner(lambda k: scatter(l, k).start())
 
     def reduce_and_gather(l):
-        each(lambda k: scatter(l, k).wait())
-
-        def add(k, total):
-            return total + land[l, k].astype(jnp.float32)
-
-        mine = acc[l, pl.ds(pl.multiple_of(me * chunk, 8), chunk), :]
-        total = (lax.fori_loop(1, n, add, mine) * scale).astype(jnp.bfloat16)
-        own[l] = total
-        fin[l, me] = total
-        each(lambda k: gather(l, k).start())
+        @pl.when(me < owners)
+        def _():
+            each(lambda k: incoming(l, k).wait_recv())
+
+            def add(k, total):
+                return total + land[l, k].astype(jnp.float32)
+
+            mine = acc[l, pl.ds(pl.multiple_of(me * chunk, 8), chunk), :]
+            total = (lax.fori_loop(1, n, add, mine) * scale).astype(jnp.bfloat16)
+            own[l] = total
+            fin[l, me] = total
+            each(lambda k: gather(l, k, me).start())
 
     def gather_finish(l):
-        each(lambda k: gathered(l, k).wait())
+        to_owner(lambda k: scatter(l, k).wait_send())
+
+        @pl.when(me < owners)
+        def _():
+            each(lambda k: gather(l, k, me).wait_send())
+
+        def arrive(k):
+            source = lax.rem(me + n - k, n)
+
+            @pl.when(source < owners)
+            def _():
+                gather(l, k, source).wait_recv()
+
+        each(arrive)
 
     rot_cot.start()
     forward(0, u0, m0)
@@ -286,8 +314,9 @@
     rows, width = tokens.shape
     layers, _, hidden = w_in.shape
     scale = 1.0 / (rows * n) ** 0.5
-    chunk = -(-2 * hidden // (8 * n)) * 8
-    cols = -(-(width + 1) // LANES) * LANES
+    needed = 2 * width + TRACK_W + 8
+    chunk = -(-needed // (8 * n)) * 8
+    owners = -(-needed // chunk)
     shifts, near, small, groups = plan(n, rows, width)
     copies = len(groups) + len(near) - len(small) + 1
     bf16, f32 = jnp.bfloat16, jnp.float32
@@ -298,21 +327,25 @@
         out_shape=[
             jax.ShapeDtypeStruct((width, rows), bf16),
             jax.ShapeDtypeStruct((width, rows), bf16),
-            jax.ShapeDtypeStruct((layers, n, chunk, cols), bf16),
+            jax.ShapeDtypeStruct((layers, owners, chunk, hidden), bf16),
         ],
-        in_specs=[vmem] * 8,
+        in_specs=[vmem] * 6,
         out_specs=[vmem] * 3,
         scratch_shapes=[block] * 7
         + [
+            pltpu.VMEM((layers, hidden, width), bf16),
+            pltpu.VMEM((layers, hidden, width), bf16),
+            pltpu.VMEM((layers, hidden, 1), f32),
+            pltpu.VMEM((layers, width, 1), f32),
             pltpu.VMEM((4, (near[-1] + 1) * TRACK_W, rows // 2), bf16),
             pltpu.VMEM((layers, hidden, rows), bf16),
             pltpu.VMEM((layers, hidden, rows), f32),
             pltpu.VMEM((hidden, rows), bf16),
-            pltpu.VMEM((layers, n * chunk, cols), f32),
-            pltpu.VMEM((layers, n, chunk, cols), bf16),
-            pltpu.VMEM((layers, n, chunk, cols), bf16),
-            pltpu.VMEM((layers, chunk, cols), bf16),
-            pltpu.VMEM((layers, n, chunk, cols), bf16),
+            pltpu.VMEM((layers, owners * chunk, hidden), f32),
+            pltpu.VMEM((layers, owners, chunk, hidden), bf16),
+            pltpu.VMEM((layers, n, chunk, hidden), bf16),
+            pltpu.VMEM((layers, chunk, hidden), bf16),
+            pltpu.VMEM((layers, owners, chunk, hidden), bf16),
             pltpu.SemaphoreType.DMA((4, copies)),
             pltpu.SemaphoreType.DMA((4, copies)),
         ]
@@ -324,20 +357,18 @@
         tokens.T,
         cotangent.T,
         w_in,
-        w_in.transpose(0, 2, 1),
-        w_out,
         w_out.transpose(0, 2, 1),
-        b_in[:, :, None],
-        b_out[:, :, None],
+        b_in,
+        b_out,
     )
-    sums = reduced.reshape(layers, n * chunk, cols).astype(f32)
+    sums = reduced.reshape(layers, owners * chunk, hidden).astype(f32)
     return (
         result.T,
         grad.T,
-        sums[:, hidden : 2 * hidden, :width].transpose(0, 2, 1),
-        sums[:, hidden : 2 * hidden, width],
-        sums[:, :hidden, :width],
-        sums[:, :width, width],
+        sums[:, width : 2 * width],
+        sums[:, 2 * width],
+        sums[:, :width].transpose(0, 2, 1),
+        sums[:, 2 * width + TRACK_W, :width],
     )
 
 

time: 194 us -> 179 us (0.923)
  the two profiles are of different devices: /device:TPU:15 before, /device:TPU:31 now
where the time goes in v1:
time: 179 us
  Pallas kernels  172 us (96%)
  local copies, waits for them, and re-layouts  5.22 us (3%)
    pallas_call x1, Pallas kernels, local(): pl.pallas_call(functools.partial(kernel, n, scale), out_shape=[jax.ShapeD...  172 us

profile of v1, /device:TPU:31, one launch (start us, length us, event | category | flops | bytes accessed | tf_op | source)
XLA Modules:
  0.0 179.2 jit_solution(11636130755710302693)
XLA Ops:
  0.6 171.6 %shard_map.109 = (bf16[320,2048]{1,0:T(8,128)(2,1)}, bf16[320,2048]{1,0:T(8,128)(2,1)}, bf16[2,28,24,640]{3,2,1,0:T(8,128)(2,1)}) custom-call(bf16[320,2048]{1,0:T(8,128)(2,1)} %bitcast.16, bf16[320,2048]{1,0:T(8,128)(2,1)} %bitcast.17, bf16[2,320,640]{2,1,0:T(8,128)(2,1)} %w_in.1, bf16[2,320,640]{2,1,0:T(8,128)(2,1)} %bitcast.20, f32[2,640]{1,0:T(2,128)} %b_in_row.1, ...), custom_call_target="tpu_custom_call" | custom-call | tf_op jit(solution)/shard_map/pallas_call | solution.py:325
  172.2 1.7 bitcast_convert_fusion
  173.9 0.6 copy.18
  174.5 0.0 copy-start.1
  174.5 1.9 %slice_bitcast_fusion = (f32[2,640,320]{1,2,0:T(8,128)}, f32[2,320,640]{2,1,0:T(8,128)}) fusion(f32[2,672,640]{2,1,0:T(8,128)S(1)} %bitcast_convert_fusion), kind=kLoop, calls=%fused_computation.1 | loop fusion | bytes 6553600 | tf_op jit(solution)/shard_map/transpose | solution.py:370
  176.4 0.0 copy-start
  176.4 0.6 copy.17
  177.0 0.0 copy-done.1
  177.0 1.1 copy.21
  178.1 0.0 copy-done
  178.1 1.1 copy.22
  (2 shorter events, 0.0 us)
Async XLA Ops:
  174.5 2.5 %copy-start.1 = (bf16[320,2048]{1,0:T(8,128)(2,1)S(1)}, bf16[320,2048]{1,0:T(8,128)(2,1)}, u32[]{:S(2)}) copy-start(bf16[320,2048]{1,0:T(8,128)(2,1)} %get-tuple-element.9) | copy-start | bytes 3932164
  176.4 1.7 copy-start

commit v2 on v1

--- a/solution.py
+++ b/solution.py
@@ -32,6 +32,17 @@
 
 def channels(first, last):
     return pl.ds(first * TRACK_W, (last - first) * TRACK_W)
+
+
+def radices(n):
+    factors = []
+    for factor in [2] + [4] * 16 + [2] * 2:
+        if n % factor == 0 and n > 1:
+            factors.append(factor)
+            n //= factor
+    if n > 1:
+        factors.append(n)
+    return factors
 
 
 class Rotation:
@@ -121,14 +132,15 @@
 def kernel(
     n, scale, u0, cot, w_in, w_out_t, b_in_row, b_out_row,
     result, grad, reduced,
-    back1, m0, u1, m1, r1, g1, back0, w_in_t, w_out, b_in, b_out,
+    back1, u1, r1, back0, w_in_t, w_out, b_in, b_out,
     halo, act, slope, delta, acc, part, land, own, fin,
     rot_send, rot_recv, rs_send, rs_recv, ag_send, ag_recv,
 ):
     me = lax.axis_index("seq")
+    m0, m1, g1 = result, result, grad
     width, rows = u0.shape
     layers, hidden, _ = w_in_t.shape
-    owners, chunk = part.shape[1:3]
+    chunk = part.shape[2]
     tile = min(TILE, rows)
     steps = rows // tile
 
@@ -201,90 +213,93 @@
 
         tiles(body)
 
-        def narrow(i, carry):
-            part[l, i] = acc[l, pl.ds(pl.multiple_of(i * chunk, 8), chunk), :].astype(jnp.bfloat16)
-            return carry
-
-        lax.fori_loop(0, owners, narrow, 0)
-
-    def scatter(l, k):
-        to = lax.rem(me + k, n)
+    stages, stride, length, first, offset = [], 1, n, 0, 0
+    for radix in radices(n):
+        digit = lax.rem(me // stride, radix)
+        share = length // radix
+        mine = first + digit * share
+        stages.append((radix, stride, digit, share, first, mine, offset))
+        first, length, stride, offset = mine, share, stride * radix, offset + (radix - 1) * share
+    last = len(stages) - 1
+
+    def rows_of(i):
+        return pl.ds(pl.multiple_of(i * chunk, 8), chunk)
+
+    def exchange(s, j, src, dst, sends, recvs):
+        radix, stride, digit = stages[s][:3]
         return pltpu.make_async_remote_copy(
-            src_ref=part.at[l, to],
-            dst_ref=land.at[l, k],
-            send_sem=rs_send.at[l, k],
-            recv_sem=rs_recv.at[l, k],
-            device_id=(to,),
+            src_ref=src,
+            dst_ref=dst,
+            send_sem=sends.at[s, j],
+            recv_sem=recvs.at[s, j],
+            device_id=(me + (lax.rem(digit + j, radix) - digit) * stride,),
             device_id_type=MESH,
         )
 
-    def incoming(l, k):
-        return pltpu.make_async_remote_copy(
-            src_ref=own.at[l],
-            dst_ref=land.at[l, k],
-            send_sem=rs_send.at[l, k],
-            recv_sem=rs_recv.at[l, k],
-            device_id=(lax.rem(me + k, n),),
-            device_id_type=MESH,
-        )
-
-    def gather(l, k, slot):
-        return pltpu.make_async_remote_copy(
-            src_ref=own.at[l],
-            dst_ref=fin.at[l, slot],
-            send_sem=ag_send.at[l, k],
-            recv_sem=ag_recv.at[l, k],
-            device_id=(lax.rem(me + k, n),),
-            device_id_type=MESH,
-        )
-
-    def each(body):
-        def step(k, carry):
-            body(k)
+    def scatter(l, s):
+        radix, _, digit, share, first, _, offset = stages[s]
+        return [
+            exchange(
+                s, j,
+                part.at[l, pl.ds(first + lax.rem(digit + j, radix) * share, share)],
+                land.at[l, pl.ds(offset + (j - 1) * share, share)],
+                rs_send.at[l], rs_recv.at[l],
+            )
+            for j in range(1, radix)
+        ]
+
+    def gather(l, s, arriving):
+        radix, _, digit, share, first, mine, _ = stages[s]
+        return [
+            exchange(
+                s, j,
+                fin.at[l, pl.ds(mine, share)],
+                fin.at[
+                    l,
+                    pl.ds(first + lax.rem(digit + radix - j, radix) * share, share)
+                    if arriving
+                    else pl.ds(mine, share),
+                ],
+                ag_send.at[l], ag_recv.at[l],
+            )
+            for j in range(1, radix)
+        ]
+
+    def scatter_start(l):
+        def narrow(i, carry):
+            part[l, i] = acc[l, rows_of(i), :].astype(jnp.bfloat16)
             return carry
 
-        lax.fori_loop(1, n, step, 0)
-
-    def to_owner(body):
-        def guarded(k):
-            @pl.when(lax.rem(me + k, n) < owners)
-            def _():
-                body(k)
-
-        each(guarded)
-
-    def scatter_start(l):
-        to_owner(lambda k: scatter(l, k).start())
-
-    def reduce_and_gather(l):
-        @pl.when(me < owners)
-        def _():
-            each(lambda k: incoming(l, k).wait_recv())
-
-            def add(k, total):
-                return total + land[l, k].astype(jnp.float32)
-
-            mine = acc[l, pl.ds(pl.multiple_of(me * chunk, 8), chunk), :]
-            total = (lax.fori_loop(1, n, add, mine) * scale).astype(jnp.bfloat16)
-            own[l] = total
-            fin[l, me] = total
-            each(lambda k: gather(l, k, me).start())
-
-    def gather_finish(l):
-        to_owner(lambda k: scatter(l, k).wait_send())
-
-        @pl.when(me < owners)
-        def _():
-            each(lambda k: gather(l, k, me).wait_send())
-
-        def arrive(k):
-            source = lax.rem(me + n - k, n)
-
-            @pl.when(source < owners)
-            def _():
-                gather(l, k, source).wait_recv()
-
-        each(arrive)
+        lax.fori_loop(0, n, narrow, 0)
+        for copy in scatter(l, 0):
+            copy.start()
+
+    def scatter_step(l, s):
+        radix, _, _, share, _, mine, offset = stages[s]
+        for copy in scatter(l, s):
+            copy.wait()
+
+        def add(i, carry):
+            total = acc[l, rows_of(mine + i), :]
+            for j in range(radix - 1):
+                total = total + land[l, offset + j * share + i].astype(jnp.float32)
+            if s < last:
+                acc[l, rows_of(mine + i), :] = total
+                part[l, mine + i] = total.astype(jnp.bfloat16)
+            else:
+                fin[l, mine + i] = (total * scale).astype(jnp.bfloat16)
+            return carry
+
+        lax.fori_loop(0, share, add, 0)
+        for copy in scatter(l, s + 1) if s < last else gather(l, last, False):
+            copy.start()
+
+    def gather_step(l, s):
+        for copy in gather(l, s, True):
+            copy.wait()
+        if s > 0:
+            for copy in gather(l, s - 1, False):
+                copy.start()
 
     rot_cot.start()
     forward(0, u0, m0)
@@ -294,19 +309,23 @@
     forward(1, u1, m1)
     backward(1, back1, g1)
     rot_g1.start()
+    weight_grads(1, u1, back1)
+    scatter_start(1)
+    rot_g1.finish()
     rot_m1.start()
-    weight_grads(1, u1, back1)
-    rot_g1.finish()
-    scatter_start(1)
     backward(0, back0, grad)
+    todo = [functools.partial(scatter_step, s=s) for s in range(last + 1)]
+    todo += [functools.partial(gather_step, s=s) for s in reversed(range(last + 1))]
+    todo[0](1)
     weight_grads(0, u0, back0)
     scatter_start(0)
+    todo[1](1)
     rot_m1.finish()
     result[...] = r1[...]
-    reduce_and_gather(1)
-    reduce_and_gather(0)
-    gather_finish(1)
-    gather_finish(0)
+    for step in range(len(todo)):
+        todo[step](0)
+        if step + 2 < len(todo):
+            todo[step + 2](1)
     reduced[...] = fin[...]
 
 
@@ -316,8 +335,8 @@
     scale = 1.0 / (rows * n) ** 0.5
     needed = 2 * width + TRACK_W + 8
     chunk = -(-needed // (8 * n)) * 8
-    owners = -(-needed // chunk)
     shifts, near, small, groups = plan(n, rows, width)
+    factors = radices(n)
     copies = len(groups) + len(near) - len(small) + 1
     bf16, f32 = jnp.bfloat16, jnp.float32
     vmem = pl.BlockSpec(memory_space=pltpu.VMEM)
@@ -327,11 +346,11 @@
         out_shape=[
             jax.ShapeDtypeStruct((width, rows), bf16),
             jax.ShapeDtypeStruct((width, rows), bf16),
-            jax.ShapeDtypeStruct((layers, owners, chunk, hidden), bf16),
+            jax.ShapeDtypeStruct((layers, n, chunk, hidden), bf16),
         ],
         in_specs=[vmem] * 6,
         out_specs=[vmem] * 3,
-        scratch_shapes=[block] * 7
+        scratch_shapes=[block] * 4
         + [
             pltpu.VMEM((layers, hidden, width), bf16),
             pltpu.VMEM((layers, hidden, width), bf16),
@@ -341,15 +360,15 @@
             pltpu.VMEM((layers, hidden, rows), bf16),
             pltpu.VMEM((layers, hidden, rows), f32),
             pltpu.VMEM((hidden, rows), bf16),
-            pltpu.VMEM((layers, owners * chunk, hidden), f32),
-            pltpu.VMEM((layers, owners, chunk, hidden), bf16),
+            pltpu.VMEM((layers, n * chunk, hidden), f32),
+            pltpu.VMEM((layers, n, chunk, hidden), bf16),
             pltpu.VMEM((layers, n, chunk, hidden), bf16),
             pltpu.VMEM((layers, chunk, hidden), bf16),
-            pltpu.VMEM((layers, owners, chunk, hidden), bf16),
+            pltpu.VMEM((layers, n, chunk, hidden), bf16),
             pltpu.SemaphoreType.DMA((4, copies)),
             pltpu.SemaphoreType.DMA((4, copies)),
         ]
-        + [pltpu.SemaphoreType.DMA((layers, n))] * 4,
+        + [pltpu.SemaphoreType.DMA((layers, len(factors), max(factors)))] * 4,
         compiler_params=pltpu.CompilerParams(
             collective_id=0, has_side_effects=True, vmem_limit_bytes=64 * 1024 * 1024 - 65536
         ),
@@ -361,7 +380,7 @@
         b_in,
         b_out,
     )
-    sums = reduced.reshape(layers, owners * chunk, hidden).astype(f32)
+    sums = reduced.reshape(layers, n * chunk, hidden).astype(f32)
     return (
         result.T,
         grad.T,

time: 179 us -> 116 us (0.65)
  the two profiles are of different devices: /device:TPU:31 before, /device:TPU:0 now
where the time goes in v2:
time: 116 us
  Pallas kernels  108 us (93%)
  local copies, waits for them, and re-layouts  5.22 us (4%)
  other arithmetic  1.8 us (2%)
    pallas_call x1, Pallas kernels, local(): pl.pallas_call(functools.partial(kernel, n, scale), out_shape=[jax.ShapeD...  108 us
    unnamed x8, local copies, waits for them, and re-layouts  3.3 us

profile of v2, /device:TPU:0, one launch (start us, length us, event | category | flops | bytes accessed | tf_op | source)
XLA Modules:
  0.0 115.5 jit_solution(1009606144561506100)
XLA Ops:
  0.6 107.8 %shard_map.109 = (bf16[320,2048]{1,0:T(8,128)(2,1)}, bf16[320,2048]{1,0:T(8,128)(2,1)}, bf16[2,32,24,640]{3,2,1,0:T(8,128)(2,1)}) custom-call(bf16[320,2048]{1,0:T(8,128)(2,1)} %bitcast.16, bf16[320,2048]{1,0:T(8,128)(2,1)} %bitcast.17, bf16[2,320,640]{2,1,0:T(8,128)(2,1)} %w_in.1, bf16[2,320,640]{2,1,0:T(8,128)(2,1)} %bitcast.20, f32[2,640]{1,0:T(2,128)} %b_in_row.1, ...), custom_call_target="tpu_custom_call" | custom-call | tf_op jit(solution)/shard_map/pallas_call | solution.py:344
  108.5 1.8 %bitcast_convert_fusion = f32[2,768,640]{2,1,0:T(8,128)S(1)} fusion(bf16[2,32,24,640]{3,2,1,0:T(8,128)(2,1)} %get-tuple-element.11), kind=kLoop, calls=%fused_computation | loop fusion | flops 983040 | bytes 5898240 | tf_op jit(solution)/shard_map/convert_element_type | solution.py:383
  110.3 0.6 copy.18
  110.9 0.0 copy-start.1
  110.9 1.9 %slice_bitcast_fusion = (f32[2,640,320]{1,2,0:T(8,128)}, f32[2,320,640]{2,1,0:T(8,128)}) fusion(f32[2,768,640]{2,1,0:T(8,128)S(1)} %bitcast_convert_fusion), kind=kLoop, calls=%fused_computation.1 | loop fusion | bytes 6553600 | tf_op jit(solution)/shard_map/transpose | solution.py:389
  112.8 0.0 copy-start
  112.8 0.6 copy.17
  113.4 0.0 copy-done.1
  113.4 1.1 copy.21
  114.5 0.0 copy-done
  114.5 1.1 copy.22
  (2 shorter events, 0.0 us)
Async XLA Ops:
  110.9 2.5 %copy-start.1 = (bf16[320,2048]{1,0:T(8,128)(2,1)S(1)}, bf16[320,2048]{1,0:T(8,128)(2,1)}, u32[]{:S(2)}) copy-start(bf16[320,2048]{1,0:T(8,128)(2,1)} %get-tuple-element.9) | copy-start | bytes 3932164
  112.8 1.7 %copy-start = (bf16[320,2048]{1,0:T(8,128)(2,1)S(1)}, bf16[320,2048]{1,0:T(8,128)(2,1)}, u32[]{:S(2)}) copy-start(bf16[320,2048]{1,0:T(8,128)(2,1)} %get-tuple-element.10) | copy-start | bytes 3932164

commit v3 on v2

--- a/solution.py
+++ b/solution.py
@@ -45,28 +45,43 @@
     return factors
 
 
+def halfway(n, groups):
+    for hops, first, last in groups:
+        if 2 * hops == n and n % 4 == 0 and last - first > 1:
+            return list(range(first, last))
+    return []
+
+
 class Rotation:
-    def __init__(self, me, n, sign, src, dst, halo, send, recv):
+    def __init__(self, me, n, sign, src, dst, halo, relay, send, recv):
         self.sign, self.src, self.dst, self.halo = sign, src, dst, halo
         width, rows = src.shape
         self.rows = rows
         self.shifts, self.near, self.small, self.groups = plan(n, rows, width)
-        self.copies = []
-
-        def add(source, target, hops):
-            k = len(self.copies)
-            self.copies.append(
+        self.copies, self.onward = [], []
+        split = halfway(n, self.groups)
+
+        def add(source, target, hops, direction=sign, into=self.copies):
+            k = len(self.copies) + len(self.onward)
+            into.append(
                 pltpu.make_async_remote_copy(
                     src_ref=source,
                     dst_ref=target,
                     send_sem=send.at[k],
                     recv_sem=recv.at[k],
-                    device_id=(lax.rem(me + (sign * hops) % n, n),),
+                    device_id=(lax.rem(me + (direction * hops) % n, n),),
                     device_id_type=MESH,
                 )
             )
 
+        for i, t in enumerate(split):
+            piece, stop = channels(t, t + 1), relay.at[channels(i, i + 1), :]
+            way = 1 if i % 2 == 0 else -1
+            add(src.at[piece, :], stop, n // 4, way)
+            add(stop, dst.at[piece, :], n // 4, way, self.onward)
         for hops, first, last in sorted(self.groups, reverse=True):
+            if first in split:
+                continue
             piece = channels(first, last)
             add(src.at[piece, :], dst.at[piece, :], hops)
         wide = [t for t in self.near if t not in self.small]
@@ -81,9 +96,19 @@
         for copy in self.copies:
             copy.start()
 
+    def pass_on(self):
+        for first, second in zip(self.copies, self.onward):
+            first.wait_recv()
+            second.start()
+
     def finish(self):
         rows, src, dst, halo = self.rows, self.src, self.dst, self.halo
-        for copy in self.copies:
+        for i, copy in enumerate(self.copies):
+            if i < len(self.onward):
+                copy.wait_send()
+            else:
+                copy.wait()
+        for copy in self.onward:
             copy.wait()
         dst[channels(0, 1), :] = src[channels(0, 1), :]
         lane = lax.broadcasted_iota(jnp.int32, (TRACK_W, LANES), 1)
@@ -133,7 +158,7 @@
     n, scale, u0, cot, w_in, w_out_t, b_in_row, b_out_row,
     result, grad, reduced,
     back1, u1, r1, back0, w_in_t, w_out, b_in, b_out,
-    halo, act, slope, delta, acc, part, land, own, fin,
+    halo, relay, act, slope, delta, acc, part, land, own, fin,
     rot_send, rot_recv, rs_send, rs_recv, ag_send, ag_recv,
 ):
     me = lax.axis_index("seq")
@@ -163,19 +188,23 @@
     pl.semaphore_wait(barrier, n - 1)
 
     def rotation(i, sign, src, dst):
-        return Rotation(me, n, sign, src, dst, halo.at[i], rot_send.at[i], rot_recv.at[i])
+        return Rotation(me, n, sign, src, dst, halo.at[i], relay.at[i], rot_send.at[i], rot_recv.at[i])
 
     rot_cot = rotation(0, -1, cot, back1)
     rot_m0 = rotation(1, 1, m0, u1)
     rot_m1 = rotation(2, 1, m1, r1)
     rot_g1 = rotation(3, -1, g1, back0)
 
-    def tiles(body):
+    def tiles(body, between=None):
         def step(i, carry):
             body(pl.ds(pl.multiple_of(i * tile, tile), tile))
             return carry
 
-        lax.fori_loop(0, steps, step, 0)
+        middle = steps // 2 if between else 0
+        if between:
+            lax.fori_loop(0, middle, step, 0)
+            between()
+        lax.fori_loop(middle, steps, step, 0)
 
     def forward(l, u, out):
         def body(cols):
@@ -200,7 +229,7 @@
 
         tiles(body)
 
-    def weight_grads(l, u, back):
+    def weight_grads(l, u, back, between=None):
         ones = jnp.ones((TRACK_W, tile), jnp.bfloat16)
 
         def body(cols):
@@ -211,7 +240,7 @@
             )
             acc[l, pl.ds(2 * width + TRACK_W, 8), pl.ds(0, width)] += dot_t(ones, b)[:8]
 
-        tiles(body)
+        tiles(body, between)
 
     stages, stride, length, first, offset = [], 1, n, 0, 0
     for radix in radices(n):
@@ -304,16 +333,19 @@
     rot_cot.start()
     forward(0, u0, m0)
     rot_m0.start()
+    rot_cot.pass_on()
+    rot_m0.pass_on()
     rot_cot.finish()
     rot_m0.finish()
     forward(1, u1, m1)
     backward(1, back1, g1)
     rot_g1.start()
-    weight_grads(1, u1, back1)
+    weight_grads(1, u1, back1, rot_g1.pass_on)
     scatter_start(1)
     rot_g1.finish()
     rot_m1.start()
     backward(0, back0, grad)
+    rot_m1.pass_on()
     todo = [functools.partial(scatter_step, s=s) for s in range(last + 1)]
     todo += [functools.partial(gather_step, s=s) for s in reversed(range(last + 1))]
     todo[0](1)
@@ -337,7 +369,7 @@
     chunk = -(-needed // (8 * n)) * 8
     shifts, near, small, groups = plan(n, rows, width)
     factors = radices(n)
-    copies = len(groups) + len(near) - len(small) + 1
+    copies = len(groups) + len(near) - len(small) + 1 + 2 * len(halfway(n, groups))
     bf16, f32 = jnp.bfloat16, jnp.float32
     vmem = pl.BlockSpec(memory_space=pltpu.VMEM)
     block = pltpu.VMEM((width, rows), bf16)
@@ -357,6 +389,9 @@
             pltpu.VMEM((layers, hidden, 1), f32),
             pltpu.VMEM((layers, width, 1), f32),
             pltpu.VMEM((4, (near[-1] + 1) * TRACK_W, rows // 2), bf16),
+            pltpu.VMEM((4, max(len(halfway(n, groups)), 1) * TRACK_W, rows), bf16)
+            if halfway(n, groups)
+            else pltpu.VMEM((4, TRACK_W, LANES), bf16),
             pltpu.VMEM((layers, hidden, rows), bf16),
             pltpu.VMEM((layers, hidden, rows), f32),
             pltpu.VMEM((hidden, rows), bf16),

time: 116 us -> 119 us (1.026)
  Pallas kernels: 108 us -> 111 us
    pallas_call x1, Pallas kernels: 108 us -> 111 us  [local(): pl.pallas_call(functools.partial(kernel, n, scale), out_shape=[jax.ShapeD...]
where the time goes in v3:
time: 119 us
  Pallas kernels  111 us (93%)
  local copies, waits for them, and re-layouts  5.22 us (4%)
  other arithmetic  1.8 us (2%)
    pallas_call x1, Pallas kernels, local(): pl.pallas_call(functools.partial(kernel, n, scale), out_shape=[jax.ShapeD...  111 us
    unnamed x8, local copies, waits for them, and re-layouts  3.3 us

profile of v3, /device:TPU:0, one launch (start us, length us, event | category | flops | bytes accessed | tf_op | source)
XLA Modules:
  0.0 118.6 jit_solution(17743405847816192547)
XLA Ops:
  0.6 110.9 %shard_map.109 = (bf16[320,2048]{1,0:T(8,128)(2,1)}, bf16[320,2048]{1,0:T(8,128)(2,1)}, bf16[2,32,24,640]{3,2,1,0:T(8,128)(2,1)}) custom-call(bf16[320,2048]{1,0:T(8,128)(2,1)} %bitcast.16, bf16[320,2048]{1,0:T(8,128)(2,1)} %bitcast.17, bf16[2,320,640]{2,1,0:T(8,128)(2,1)} %w_in.1, bf16[2,320,640]{2,1,0:T(8,128)(2,1)} %bitcast.20, f32[2,640]{1,0:T(2,128)} %b_in_row.1, ...), custom_call_target="tpu_custom_call" | custom-call | tf_op jit(solution)/shard_map/pallas_call | solution.py:376
  111.6 1.8 %bitcast_convert_fusion = f32[2,768,640]{2,1,0:T(8,128)S(1)} fusion(bf16[2,32,24,640]{3,2,1,0:T(8,128)(2,1)} %get-tuple-element.11), kind=kLoop, calls=%fused_computation | loop fusion | flops 983040 | bytes 5898240 | tf_op jit(solution)/shard_map/convert_element_type | solution.py:418
  113.4 0.6 copy.18
  114.0 0.0 copy-start.1
  114.0 1.9 %slice_bitcast_fusion = (f32[2,640,320]{1,2,0:T(8,128)}, f32[2,320,640]{2,1,0:T(8,128)}) fusion(f32[2,768,640]{2,1,0:T(8,128)S(1)} %bitcast_convert_fusion), kind=kLoop, calls=%fused_computation.1 | loop fusion | bytes 6553600 | tf_op jit(solution)/shard_map/transpose | solution.py:424
  115.9 0.0 copy-start
  115.9 0.6 copy.17
  116.5 0.0 copy-done.1
  116.5 1.1 copy.21
  117.5 0.0 copy-done
  117.5 1.1 copy.22
  (2 shorter events, 0.0 us)
Async XLA Ops:
  114.0 2.5 %copy-start.1 = (bf16[320,2048]{1,0:T(8,128)(2,1)S(1)}, bf16[320,2048]{1,0:T(8,128)(2,1)}, u32[]{:S(2)}) copy-start(bf16[320,2048]{1,0:T(8,128)(2,1)} %get-tuple-element.9) | copy-start | bytes 3932164
  115.9 1.7 %copy-start = (bf16[320,2048]{1,0:T(8,128)(2,1)S(1)}, bf16[320,2048]{1,0:T(8,128)(2,1)}, u32[]{:S(2)}) copy-start(bf16[320,2048]{1,0:T(8,128)(2,1)} %get-tuple-element.10) | copy-start | bytes 3932164

commit v4 on v2

--- a/solution.py
+++ b/solution.py
@@ -153,13 +153,6 @@
         return carry
 
     lax.fori_loop(1, n, greet, 0)
-    acc[...] = jnp.zeros_like(acc)
-    for l in range(layers):
-        w_in_t[l] = w_in[l].T
-        w_out[l] = w_out_t[l].T
-        for row, column in ((b_in_row, b_in), (b_out_row, b_out)):
-            spread = jnp.broadcast_to(row[l : l + 1, :], (LANES, row.shape[1]))
-            column[l] = spread.T[:, :1]
     pl.semaphore_wait(barrier, n - 1)
 
     def rotation(i, sign, src, dst):
@@ -302,8 +295,18 @@
                 copy.start()
 
     rot_cot.start()
+    w_in_t[0] = w_in[0].T
+    for l in range(layers):
+        for row, column in ((b_in_row, b_in), (b_out_row, b_out)):
+            spread = jnp.broadcast_to(row[l : l + 1, :], (LANES, row.shape[1]))
+            column[l] = spread.T[:, :1]
     forward(0, u0, m0)
     rot_m0.start()
+    for l in range(1, layers):
+        w_in_t[l] = w_in[l].T
+    for l in range(layers):
+        w_out[l] = w_out_t[l].T
+    acc[...] = jnp.zeros_like(acc)
     rot_cot.finish()
     rot_m0.finish()
     forward(1, u1, m1)
@@ -380,14 +383,14 @@
         b_in,
         b_out,
     )
-    sums = reduced.reshape(layers, n * chunk, hidden).astype(f32)
+    sums = reduced.reshape(layers, n * chunk, hidden)
     return (
         result.T,
         grad.T,
-        sums[:, width : 2 * width],
-        sums[:, 2 * width],
-        sums[:, :width].transpose(0, 2, 1),
-        sums[:, 2 * width + TRACK_W, :width],
+        sums[:, width : 2 * width].astype(f32),
+        sums[:, 2 * width].astype(f32),
+        sums[:, :width].transpose(0, 2, 1).astype(f32),
+        sums[:, 2 * width + TRACK_W, :width].astype(f32),
     )
 
 

time: 116 us -> 118 us (1.017)
  other arithmetic: 1.8 us -> 4.72 us
    convert_element_type x1 -> x3, other arithmetic: 1.8 us -> 4.72 us  [the longest x1 3.41 us: local(): sums[:, :width].transpose(0, 2, 1).astype(f32)]
    transpose x1 -> x0, local copies, waits for them, and re-layouts: 1.91 us -> none  [local(): sums[:, :width].transpose(0, 2, 1)]
    unnamed x8 -> x7, local copies, waits for them, and re-layouts: 3.3 us -> 3.44 us
where the time goes in v4:
time: 118 us; the launch traced here: 117 us
  Pallas kernels  108 us (92%)
  other arithmetic  4.72 us (4%)
  local copies, waits for them, and re-layouts  4.15 us (4%)
    pallas_call x1, Pallas kernels, local(): pl.pallas_call(functools.partial(kernel, n, scale), out_shape=[jax.ShapeD...  108 us
    unnamed x7, local copies, waits for them, and re-layouts  3.44 us
    convert_element_type x1, other arithmetic, local(): sums[:, :width].transpose(0, 2, 1).astype(f32)  3.41 us

profile of v4, /device:TPU:0, one launch (start us, length us, event | category | flops | bytes accessed | tf_op | source)
XLA Modules:
  0.0 117.4 jit_solution(3340736058573607876)
XLA Ops:
  0.6 107.8 %shard_map.109 = (bf16[320,2048]{1,0:T(8,128)(2,1)}, bf16[320,2048]{1,0:T(8,128)(2,1)}, bf16[2,32,24,640]{3,2,1,0:T(8,128)(2,1)}) custom-call(bf16[320,2048]{1,0:T(8,128)(2,1)} %bitcast.19, bf16[320,2048]{1,0:T(8,128)(2,1)} %bitcast.20, bf16[2,320,640]{2,1,0:T(8,128)(2,1)} %w_in.1, bf16[2,320,640]{2,1,0:T(8,128)(2,1)} %bitcast.23, f32[2,640]{1,0:T(2,128)} %b_in_row.1, ...), custom_call_target="tpu_custom_call" | custom-call | tf_op jit(solution)/shard_map/pallas_call | solution.py:347
  108.5 0.7 slice.19
  109.2 0.6 fusion
  109.8 0.7 slice_convert_fusion.1
  110.5 0.6 copy.19
  111.1 0.0 copy-start.1
  111.1 3.4 %convert_bitcast_fusion = (f32[2,640,320]{1,2,0:T(8,128)}, f32[2,320,640]{2,1,0:T(8,128)}) fusion(bf16[2,768,640]{2,1,0:T(8,128)(2,1)} %bitcast.18), kind=kLoop, calls=%fused_computation | loop fusion | flops 819200 | bytes 4915200 | tf_op jit(solution)/shard_map/convert_element_type | solution.py:392
  114.5 0.0 copy-start
  114.5 0.0 copy-done.1
  114.5 1.1 copy.22
  115.6 0.7 copy-done
  116.3 1.1 copy.23
Async XLA Ops:
  111.1 3.4 %copy-start.1 = (bf16[320,2048]{1,0:T(8,128)(2,1)S(1)}, bf16[320,2048]{1,0:T(8,128)(2,1)}, u32[]{:S(2)}) copy-start(bf16[320,2048]{1,0:T(8,128)(2,1)} %get-tuple-element.9) | copy-start | bytes 3932164
  114.5 1.8 %copy-start = (bf16[320,2048]{1,0:T(8,128)(2,1)S(1)}, bf16[320,2048]{1,0:T(8,128)(2,1)}, u32[]{:S(2)}) copy-start(bf16[320,2048]{1,0:T(8,128)(2,1)} %get-tuple-element.10) | copy-start | bytes 3932164
